TPU v7x, 128 devices: a whole 4x4x4 slice. The times are simulated.
128 devices in a mesh: row: 8 (over y_lo, x), col: 16 (over z, y_hi, core).
Axes of the slice: x: 4, y: 4 (y_hi: 2, y_lo: 2; y = y_hi * 2 + y_lo), z: 4, core: 2. Of those that a mesh axis runs over, the one named last changes fastest.
Arguments:
- sources: bfloat16 [64, 32768], P(None, ('row', 'col')), may hold values from -6 to 6
- near_tiles: bfloat16 [128, 128, 256, 256], P('row', 'col'), may hold values from -0.03125 to 0.03125
- far_left: bfloat16 [128, 128, 32, 256], P('row', 'col'), may hold values from -1 to 1
- far_right: bfloat16 [128, 128, 32, 256], P('row', 'col'), may hold values from -0.03125 to 0.03125
- pattern: int32 [128, 128], P('row', 'col'), may hold values from 0 to 2
- band_end: int32 [128], P('row'), may hold values from 0 to 127, as said below
Outputs:
- image: float32 [64, 32768], P(None, ('row', 'col'))
Inputs may be any that keep to these rules, and one draw needn't show every extreme that they name: band_end[I] is at least I, so the band of every block-row starts at its own cluster; the bands of block-rows 0 to 15 run to the last cluster.
All inputs are finite; a program needn't handle non-finite values.
Results may differ from a plain program's by a relative error of at most 0.0021.
Values may be sent and summed in bfloat16 or wider, within the bound.
A program may use at most 128 MiB of HBM per device.

v0:
```python
import jax
import jax.numpy as jnp
from jax import lax
from jax.sharding import PartitionSpec as P


def shards(sources, near_tiles, far_left, far_right, pattern, band_end):
    row_count = lax.axis_size("row")
    col_count = lax.axis_size("col")
    row_index = lax.axis_index("row")
    col_index = lax.axis_index("col")
    num_cases = sources.shape[0]
    block_size = sources.shape[1]
    row_src = lax.all_gather(sources, "col", axis=1, tiled=True).reshape(
        num_cases, col_count, block_size
    )
    col_src = lax.all_gather(sources, "row", axis=1, tiled=True).reshape(
        num_cases, row_count, block_size
    )
    row_ids = row_index * col_count + jnp.arange(col_count, dtype=jnp.int32)
    col_ids = jnp.arange(row_count, dtype=jnp.int32) * col_count + col_index
    live = (row_ids[:, None] <= col_ids[None, :]) & (col_ids[None, :] <= band_end[:, None])
    near_mask = jnp.where(live & (pattern == 1), 1.0, 0.0).astype(jnp.float32)
    far_mask = jnp.where(live & (pattern == 2), 1.0, 0.0).astype(jnp.float32)
    near_rows = jnp.einsum(
        "ikab,ckb->cika", near_tiles, col_src, preferred_element_type=jnp.float32
    )
    far_coef = jnp.einsum(
        "ikrb,ckb->ikcr", far_right, col_src, preferred_element_type=jnp.float32
    ).astype(jnp.bfloat16)
    far_rows = jnp.einsum("ikra,ikcr->cika", far_left, far_coef, preferred_element_type=jnp.float32)
    row_part = jnp.sum(
        near_rows * near_mask[None, :, :, None] + far_rows * far_mask[None, :, :, None], axis=2
    )
    near_cols = jnp.einsum(
        "ikab,cia->ckib", near_tiles, row_src, preferred_element_type=jnp.float32
    )
    back_coef = jnp.einsum(
        "ikra,cia->ikcr", far_left, row_src, preferred_element_type=jnp.float32
    ).astype(jnp.bfloat16)
    far_cols = jnp.einsum(
        "ikrb,ikcr->ckib", far_right, back_coef, preferred_element_type=jnp.float32
    )
    col_part = jnp.sum(
        near_cols * near_mask.T[None, :, :, None] + far_cols * far_mask.T[None, :, :, None], axis=2
    )
    whole = jnp.zeros((num_cases, row_count, col_count, block_size), jnp.float32)
    whole = lax.dynamic_update_index_in_dim(whole, row_part, row_index, 1)
    column_hit = jnp.arange(col_count, dtype=jnp.int32)[None, None, :, None] == col_index
    whole = whole + jnp.where(column_hit, col_part[:, :, None, :], 0.0)
    result = lax.psum_scatter(
        whole.reshape(num_cases, row_count * col_count * block_size),
        ("row", "col"),
        scatter_dimension=1,
        tiled=True,
    )
    return result


def solution(mesh):
    placed = (
        P(None, ("row", "col")),
        P("row", "col", None, None),
        P("row", "col", None, None),
        P("row", "col", None, None),
        P("row", "col"),
        P("row"),
    )
    return jax.shard_map(
        shards, mesh=mesh, in_specs=placed, out_specs=P(None, ("row", "col")), check_vma=False
    )
```

profile of v0, /device:TPU:0, one launch (start us, length us, event | category | flops | bytes accessed | tf_op | source)
XLA Modules:
  0.0 760.8 jit_solution(4454899091737025960)
XLA Ops:
  6.5 0.0 copy-start
  6.5 0.0 reduce-scatter.2.cloned.1.call-start
  6.6 29.3 %all_gather.7 = bf16[64,2048]{1,0:T(8,128)(2,1)S(1)} all-gather(bf16[64,256]{1,0:T(8,128)(2,1)} %param.6), channel_id=1, replica_groups=mesh['row'=8,'col'=16] {'row'}, dimensions={1}, use_global_device_ids=true | all-gather | bytes 294912 | tf_op jit(solution)/shard_map/all_gather | solution.py:17
  35.8 27.8 %all_gather.6 = bf16[64,4096]{1,0:T(8,128)(2,1)S(1)} all-gather(bf16[64,256]{1,0:T(8,128)(2,1)} %param.6), channel_id=1, replica_groups=mesh['row'=8,'col'=16] {'col'}, dimensions={1}, use_global_device_ids=true | all-gather | bytes 557056 | tf_op jit(solution)/shard_map/all_gather | solution.py:14
  63.7 0.8 and_select_fusion.1
  64.4 0.1 copy.37
  64.5 0.1 copy.33
  64.6 0.1 copy.58
  64.6 0.1 copy.57
  64.7 11.9 %fusion.18 = f32[16,64,8,256]{3,1,2,0:T(8,128)} fusion(bf16[16,8,256,256]{3,2,1,0:T(8,128)(2,1)} %param.7, bf16[64,16,256,1]{2,1,0,3:T(8,128)(2,1)S(1)} %bitcast.59), kind=kOutput, calls=%fused_computation.22 | convolution fusion | flops 1073741824 | bytes 25690112 | tf_op jit(solution)/shard_map/ikab,cia->ckib/dot_general | solution.py:35
  76.6 14.1 %fusion = f32[8,64,16,256]{3,1,2,0:T(8,128)} fusion(bf16[16,8,256,256]{3,2,1,0:T(8,128)(2,1)} %param.7, bf16[64,8,256,1]{2,1,0,3:T(8,128)(2,1)S(1)} %bitcast.64), kind=kOutput, calls=%fused_computation | convolution fusion | flops 1073741824 | bytes 25427968 | tf_op jit(solution)/shard_map/ikab,ckb->cika/dot_general | solution.py:25
  90.7 0.0 copy-start.1
  90.7 0.0 copy-done
  90.7 0.7 fusion.11
  91.4 0.0 slice-start
  91.4 2.4 fusion.10
  93.9 0.0 copy-done.1
  93.9 0.0 slice-start.1
  93.9 4.8 fusion.3
  98.7 1.2 broadcast_select_fusion
  99.8 0.0 slice-done
  99.8 0.0 slice-done.1
  99.8 2.7 fusion.2
  102.5 0.2 fusion.14
  102.8 3.9 copy.59
  106.7 0.0 reduce-scatter.2.cloned.1.call-update
  106.7 647.2 %reduce-scatter.2.cloned.1.call-done = f32[64,256]{1,0:T(8,128)} async-done(((f32[64,32768]{1,0:T(8,128)}), f32[64,256]{1,0:T(8,128)}) %reduce-scatter.2.cloned.1.call-update) | async-done | bytes 65552 | tf_op jit(solution)/shard_map/reduce_scatter | solution.py:51
  (4 shorter events, 0.0 us)
Async XLA Ops:
  6.5 84.2 %copy-start = (bf16[16,8,32,256]{3,2,1,0:T(8,128)(2,1)S(1)}, bf16[16,8,32,256]{3,2,1,0:T(8,128)(2,1)}, u32[]{:S(2)}) copy-start(bf16[16,8,32,256]{3,2,1,0:T(8,128)(2,1)} %param.8) | copy-start | bytes 6291460
  6.5 747.4 %reduce-scatter.2.cloned.1.call-start = ((), (), s32[]{:S(2)}) async-start(), calls=%async_computation.1 | async-start | bytes 8454144 | tf_op jit(solution)/shard_map/reduce_scatter | solution.py:51
  90.7 3.2 copy-start.1
  91.4 8.4 %slice-start = ((s8[8388608]{0:T(1024)(128)(4,1)}), s8[4194304]{0:T(1024)(128)(4,1)S(1)}, s32[]{:S(2)}) async-start(s8[8388608]{0:T(1024)(128)(4,1)} %bitcast.56), calls=%async_computation.2 | async-start | bytes 8388608
  93.9 5.9 slice-start.1
Sparse Core Ops, SparseCore 0:
  106.9 647.0 reduce-scatter.1
where the time goes:
time: 761 us
  waiting for transfers between devices  647 us (85%)
  blocking collectives  57.1 us (8%)
  matrix products  36.5 us (5%)
  between operations  13.5 us (2%)
    reduce_scatter x1, waiting for transfers between devices, shards(): lax.psum_scatter(whole.reshape(num_cases, row_count * col_count * block_s...  647 us
    all_gather x1, blocking collectives, shards(): lax.all_gather(sources, 'row', axis=1, tiled=True)  29.3 us
    all_gather x1, blocking collectives, shards(): lax.all_gather(sources, 'col', axis=1, tiled=True)  27.8 us
  transfers between devices with their start and end apart: 1, of which 1 were waited for; matrix products, arithmetic and copies ran while one was open for 0% of the time, Pallas kernels for 0%

commit v1 on v0

v1 whole, which is shorter than its diff:
```python
import functools

import jax
import jax.numpy as jnp
from jax import lax
from jax.experimental import pallas as pl
from jax.experimental.pallas import tpu as pltpu
from jax.sharding import PartitionSpec as P

MESH = pl.DeviceIdType.MESH
F32 = jnp.float32
BF16 = jnp.bfloat16
LANES = 128


def dot_nt(a, b):
    return lax.dot_general(a, b, (((1,), (1,)), ((), ())), preferred_element_type=F32)


def dot_nn(a, b):
    return lax.dot_general(a, b, (((1,), (0,)), ((), ())), preferred_element_type=F32)


def kernel(
    src_hbm, near_hbm, left_hbm, right_hbm, pat_ref, band_ref, out_ref,
    tiles, left, right, own, row_src, col_src, fwd, bwd, row_send, row_recv, col_send, col_recv,
    own_sem, near_sem, far_sem, gr_send, gr_recv, gc_send, gc_recv, rr_send, rr_recv, rc_send, rc_recv,
):
    n_row, n_col = near_hbm.shape[1], near_hbm.shape[0]
    rank = left_hbm.shape[2]
    per = LANES // rank
    row, col = lax.axis_index("row"), lax.axis_index("col")

    own_copy = pltpu.make_async_copy(src_hbm, own, own_sem)
    own_copy.start()
    right_copy = pltpu.make_async_copy(right_hbm, right, far_sem.at[0])
    left_copy = pltpu.make_async_copy(left_hbm, left, far_sem.at[1])
    right_copy.start()
    left_copy.start()

    def near_copy(i):
        return pltpu.make_async_copy(near_hbm.at[i], tiles.at[i], near_sem.at[i])

    for i in range(n_col):
        near_copy(i).start()

    barrier = pltpu.get_barrier_semaphore()

    @pl.loop(1, n_col)
    def _(d):
        pl.semaphore_signal(
            barrier, inc=1, device_id={"col": lax.rem(col + d, n_col)}, device_id_type=MESH
        )

    @pl.loop(1, n_row)
    def _(d):
        pl.semaphore_signal(
            barrier, inc=1, device_id={"row": lax.rem(row + d, n_row)}, device_id_type=MESH
        )

    pl.semaphore_wait(barrier, n_col + n_row - 2)

    def to_row(k, src, dst, send, recv):
        return pltpu.make_async_remote_copy(
            src_ref=src, dst_ref=dst, send_sem=send, recv_sem=recv,
            device_id={"row": k}, device_id_type=MESH,
        )

    def to_col(c, src, dst, send, recv):
        return pltpu.make_async_remote_copy(
            src_ref=src, dst_ref=dst, send_sem=send, recv_sem=recv,
            device_id={"col": c}, device_id_type=MESH,
        )

    own_copy.wait()

    @pl.loop(0, row)
    def _(k):
        to_row(k, own, col_src.at[row], gc_send.at[k], gc_recv.at[row]).start()

    @pl.loop(1, n_col)
    def _(d):
        c = lax.rem(col + d, n_col)
        to_col(c, own, row_src.at[col], gr_send.at[c], gr_recv.at[col]).start()

    col_src[row] = own[...]
    row_src[col] = own[...]

    @pl.loop(0, row)
    def _(k):
        col_src[k] = jnp.zeros_like(own)

    def weight(i, k, kind):
        big_i, big_j = row * n_col + i, k * n_col + col
        ok = (big_i <= big_j) & (big_j <= band_ref[i]) & (pat_ref[i, k] == kind)
        return jnp.where(ok, 1.0, 0.0).astype(F32)

    lane = lax.broadcasted_iota(jnp.int32, (1, LANES), 1) // rank
    num_cases = own.shape[0]
    wide_lane = lax.broadcasted_iota(jnp.int32, (num_cases, LANES), 1) // rank

    def lay(parts, place):
        total = parts[-1]
        for p in range(per - 1):
            total = jnp.where(place == p, parts[p], total)
        return total

    @pl.loop(row + 1, n_row)
    def _(k):
        to_row(row, own, col_src.at[k], gc_send.at[row], gc_recv.at[k]).wait_recv()

    right_copy.wait()
    pairs = n_col // per // 2

    @pl.loop(0, n_row // per)
    def _(kk):
        @pl.loop(0, pairs)
        def _(gp):
            coef = []
            for s in range(per):
                k = kk * per + s
                rows = [
                    right[(gp * 2 + g) * per + (p - s) % per, k] for g in range(2) for p in range(per)
                ]
                coef.append(dot_nt(col_src[k], jnp.concatenate(rows, axis=0)))
            for g in range(2):
                for t in range(per):
                    i = (gp * 2 + g) * per + t
                    piece = lay(
                        [coef[(p - t) % per][:, g * LANES:(g + 1) * LANES] for p in range(per)],
                        wide_lane,
                    )
                    keep = lay(
                        [jnp.full((1, LANES), weight(i, kk * per + (p - t) % per, 2), F32) for p in range(per)],
                        lane,
                    )
                    fwd[i, kk] = (piece * keep).astype(BF16)

    left_copy.wait()

    def left_rows(i):
        return jnp.concatenate(
            [
                left[i, kk * per + lax.rem(p - i + n_col, per)]
                for kk in range(n_row // per)
                for p in range(per)
            ],
            axis=0,
        )

    @pl.loop(0, n_col)
    def _(i):
        near_copy(i).wait()
        acc = dot_nn(
            jnp.concatenate([fwd[i, kk] for kk in range(n_row // per)], axis=1), left_rows(i)
        )
        for k in range(n_row):
            acc += dot_nt(col_src[k] * weight(i, k, 1).astype(BF16), tiles[i, k])

        @pl.when(i == col)
        def _():
            out_ref[...] = acc

        @pl.when(i != col)
        def _():
            row_send[i] = acc.astype(BF16)
            to_col(i, row_send.at[i], row_recv.at[col], rr_send.at[i], rr_recv.at[col]).start()

    @pl.loop(1, n_col)
    def _(d):
        c = lax.rem(col + d, n_col)
        to_col(col, own, row_src.at[c], gr_send.at[col], gr_recv.at[c]).wait_recv()

    @pl.loop(0, n_col // per)
    def _(g):
        back = [dot_nt(row_src[g * per + t], left_rows(g * per + t)) for t in range(per)]
        for kk in range(n_row // per):
            for s in range(per):
                k = kk * per + s
                piece = lay(
                    [back[(p - s) % per][:, kk * LANES:(kk + 1) * LANES] for p in range(per)],
                    wide_lane,
                )
                keep = lay(
                    [jnp.full((1, LANES), weight(g * per + (p - s) % per, k, 2), F32) for p in range(per)],
                    lane,
                )
                bwd[k, g] = (piece * keep).astype(BF16)

    @pl.loop(0, n_row - row)
    def _(step):
        k = n_row - 1 - step
        acc = jnp.zeros((num_cases, own.shape[1]), F32)
        for h in range(n_col // per // 2):
            rows = [
                right[(h * 2 + g) * per + lax.rem(p - k + n_row, per), k]
                for g in range(2)
                for p in range(per)
            ]
            acc += dot_nn(
                jnp.concatenate([bwd[k, h * 2], bwd[k, h * 2 + 1]], axis=1),
                jnp.concatenate(rows, axis=0),
            )
        for i in range(n_col):
            acc += dot_nn(row_src[i] * weight(i, k, 1).astype(BF16), tiles[i, k])

        @pl.when(k == row)
        def _():
            out_ref[...] += acc

        @pl.when(k != row)
        def _():
            col_send[k] = acc.astype(BF16)
            to_row(k, col_send.at[k], col_recv.at[row], rc_send.at[k], rc_recv.at[row]).start()

    @pl.loop(1, n_col)
    def _(d):
        c = lax.rem(col + d, n_col)
        to_col(col, own, row_recv.at[c], rr_send.at[col], rr_recv.at[c]).wait_recv()
        out_ref[...] += row_recv[c].astype(F32)

    @pl.loop(0, row)
    def _(k):
        to_row(row, own, col_recv.at[k], rc_send.at[row], rc_recv.at[k]).wait_recv()
        out_ref[...] += col_recv[k].astype(F32)

    @pl.loop(1, n_col)
    def _(d):
        c = lax.rem(col + d, n_col)
        to_col(c, own, row_src.at[col], gr_send.at[c], gr_recv.at[col]).wait_send()
        to_col(c, row_send.at[c], row_recv.at[col], rr_send.at[c], rr_recv.at[col]).wait_send()

    @pl.loop(0, row)
    def _(k):
        to_row(k, own, col_src.at[row], gc_send.at[k], gc_recv.at[row]).wait_send()

    @pl.loop(row + 1, n_row)
    def _(k):
        to_row(k, col_send.at[k], col_recv.at[row], rc_send.at[k], rc_recv.at[row]).wait_send()


def shards(sources, near_tiles, far_left, far_right, pattern, band_end):
    n_col, n_row, size = near_tiles.shape[:3]
    rank = far_left.shape[2]
    cases = sources.shape[0]
    per = LANES // rank
    dma = pltpu.SemaphoreType.DMA
    hbm = pl.BlockSpec(memory_space=pltpu.HBM)
    smem = pl.BlockSpec(memory_space=pltpu.SMEM)
    return pl.pallas_call(
        kernel,
        out_shape=jax.ShapeDtypeStruct((cases, size), F32),
        in_specs=[hbm, hbm, hbm, hbm, smem, smem],
        out_specs=pl.BlockSpec(memory_space=pltpu.VMEM),
        scratch_shapes=[
            pltpu.VMEM(near_tiles.shape, BF16),
            pltpu.VMEM(far_left.shape, BF16),
            pltpu.VMEM(far_right.shape, BF16),
            pltpu.VMEM((cases, size), BF16),
            pltpu.VMEM((n_col, cases, size), BF16),
            pltpu.VMEM((n_row, cases, size), BF16),
            pltpu.VMEM((n_col, n_row // per, cases, LANES), BF16),
            pltpu.VMEM((n_row, n_col // per, cases, LANES), BF16),
            pltpu.VMEM((n_col, cases, size), BF16),
            pltpu.VMEM((n_col, cases, size), BF16),
            pltpu.VMEM((n_row, cases, size), BF16),
            pltpu.VMEM((n_row, cases, size), BF16),
            dma,
            dma((n_col,)),
            dma((2,)),
            dma((n_col,)), dma((n_col,)),
            dma((n_row,)), dma((n_row,)),
            dma((n_col,)), dma((n_col,)),
            dma((n_row,)), dma((n_row,)),
        ],
        compiler_params=pltpu.CompilerParams(
            collective_id=0, has_side_effects=True, vmem_limit_bytes=40 * 1024 * 1024
        ),
        name="panels",
    )(sources, near_tiles, far_left, far_right, pattern, band_end)


def solution(mesh):
    placed = (
        P(None, ("row", "col")),
        P("row", "col", None, None),
        P("row", "col", None, None),
        P("row", "col", None, None),
        P("row", "col"),
        P("row"),
    )
    return jax.shard_map(
        shards, mesh=mesh, in_specs=placed, out_specs=P(None, ("row", "col")), check_vma=False
    )
```

time: 761 us -> 38 us (0.05)
  the two profiles are of different devices: /device:TPU:0 before, /device:TPU:2 now
where the time goes in v1:
time: 38 us; the launch traced here: 37.7 us
  Pallas kernels  31.7 us (83%)
  local copies, waits for them, and re-layouts  5.98 us (16%)
    pallas_call x1, Pallas kernels, shards(): pl.pallas_call(kernel, out_shape=jax.ShapeDtypeStruct((cases, size), F32)...  31.7 us
    unnamed x10, local copies, waits for them, and re-layouts  5.98 us

profile of v1, /device:TPU:2, one launch (start us, length us, event | category | flops | bytes accessed | tf_op | source)
XLA Modules:
  0.0 37.7 jit_solution(12351869899309031838)
XLA Ops:
  0.0 0.8 %copy.7.pat_ref = s32[16,8]{1,0:T(8,128)S(1)} copy(s32[16,8]{0,1:T(8,128)} %param.10) | data formatting | bytes 1024 | tf_op args[4]
  0.8 0.0 copy-start
  0.8 1.6 %copy-done = bf16[16,8,32,256]{3,2,1,0:T(8,128)(2,1)S(1)} copy-done((bf16[16,8,32,256]{3,2,1,0:T(8,128)(2,1)S(1)}, bf16[16,8,32,256]{3,2,1,0:T(8,128)(2,1)}, u32[]{:S(2)}) %copy-start) | copy-done | bytes 2097176
  2.3 0.0 copy-start.1
  2.4 1.6 %copy-done.1 = bf16[16,8,32,256]{3,2,1,0:T(8,128)(2,1)S(1)} copy-done((bf16[16,8,32,256]{3,2,1,0:T(8,128)(2,1)S(1)}, bf16[16,8,32,256]{3,2,1,0:T(8,128)(2,1)}, u32[]{:S(2)}) %copy-start.1) | copy-done | bytes 2097176
  3.9 0.0 copy-start.2
  3.9 0.8 %copy-done.2 = bf16[64,256]{1,0:T(8,128)(2,1)S(1)} copy-done((bf16[64,256]{1,0:T(8,128)(2,1)S(1)}, bf16[64,256]{1,0:T(8,128)(2,1)}, u32[]{:S(2)}) %copy-start.2) | copy-done | bytes 32792
  4.7 0.0 copy-start.3
  4.7 0.7 %copy-done.3 = s32[16]{0:T(128)S(1)} copy-done((s32[16]{0:T(128)S(1)}, s32[16]{0:T(128)}, u32[]{:S(2)}) %copy-start.3) | copy-done | bytes 88
  5.4 31.7 %panels.1 = f32[64,256]{1,0:T(8,128)S(1)} custom-call(bf16[64,256]{1,0:T(8,128)(2,1)S(1)} %copy-done.2, bf16[16,8,256,256]{3,2,1,0:T(8,128)(2,1)} %near_hbm.1, bf16[16,8,32,256]{3,2,1,0:T(8,128)(2,1)S(1)} %copy-done, bf16[16,8,32,256]{3,2,1,0:T(8,128)(2,1)S(1)} %copy-done.1, s32[16,8]{1,0:T(8,128)S(1)} %copy.7.pat_ref, s32[16]{0:T(128)S(1)} %copy-done.3), custom_call_target="tpu_custom_call" | custom-call | tf_op jit(solution)/shard_map/panels/pallas_call | solution.py:250
  37.0 0.6 %copy.9 = f32[64,256]{1,0:T(8,128)} copy(f32[64,256]{1,0:T(8,128)S(1)} %panels.1) | data formatting | bytes 131072
Async XLA Ops:
  0.8 1.6 %copy-start = (bf16[16,8,32,256]{3,2,1,0:T(8,128)(2,1)S(1)}, bf16[16,8,32,256]{3,2,1,0:T(8,128)(2,1)}, u32[]{:S(2)}) copy-start(bf16[16,8,32,256]{3,2,1,0:T(8,128)(2,1)} %left_hbm.1) | copy-start | bytes 6291460
  2.3 1.6 %copy-start.1 = (bf16[16,8,32,256]{3,2,1,0:T(8,128)(2,1)S(1)}, bf16[16,8,32,256]{3,2,1,0:T(8,128)(2,1)}, u32[]{:S(2)}) copy-start(bf16[16,8,32,256]{3,2,1,0:T(8,128)(2,1)} %right_hbm.1) | copy-start | bytes 6291460
  3.9 0.8 %copy-start.2 = (bf16[64,256]{1,0:T(8,128)(2,1)S(1)}, bf16[64,256]{1,0:T(8,128)(2,1)}, u32[]{:S(2)}) copy-start(bf16[64,256]{1,0:T(8,128)(2,1)} %src_hbm.1) | copy-start | bytes 98308
  4.7 0.7 %copy-start.3 = (s32[16]{0:T(128)S(1)}, s32[16]{0:T(128)}, u32[]{:S(2)}) copy-start(s32[16]{0:T(128)} %band_ref.1) | copy-start | bytes 196

commit v2 on v1

v2 whole, which is shorter than its diff:
```python
import functools

import jax
import jax.numpy as jnp
from jax import lax
from jax.experimental import pallas as pl
from jax.experimental.pallas import tpu as pltpu
from jax.sharding import PartitionSpec as P

MESH = pl.DeviceIdType.MESH
F32 = jnp.float32
BF16 = jnp.bfloat16
LANES = 128


def dot_nt(a, b):
    return lax.dot_general(a, b, (((1,), (1,)), ((), ())), preferred_element_type=F32)


def dot_nn(a, b):
    return lax.dot_general(a, b, (((1,), (0,)), ((), ())), preferred_element_type=F32)


def kernel(
    src_hbm, near_hbm, left_hbm, right_hbm, pat_ref, band_ref, out_ref,
    tiles, turned, left, right, own, row_src, col_src, fwd, bwd, fwd_keep, bwd_keep, near_keep,
    pair_send, pair_recv, row_send, row_recv, col_send, col_recv,
    own_sem, near_sem, far_sem, gr_send, gr_recv, gc_send, gc_recv,
    pa_send, pa_recv, rr_send, rr_recv, rc_send, rc_recv,
):
    n_row, n_col = near_hbm.shape[1], near_hbm.shape[0]
    rank = left_hbm.shape[2]
    num_cases, size = own.shape
    per = LANES // rank
    chips = n_col // 2
    planes = n_col // 4
    row, col = lax.axis_index("row"), lax.axis_index("col")
    core, chip = lax.rem(col, 2), col // 2
    partner = col + 1 - 2 * core

    def other(c, d):
        return lax.rem(c + 2 * d, n_col)

    barrier = pltpu.get_barrier_semaphore()

    def greet(device):
        pl.semaphore_signal(barrier, inc=1, device_id=device, device_id_type=MESH)

    for d in range(1, n_row):
        greet({"row": lax.rem(row + d, n_row)})
    for d in range(1, chips):
        greet({"col": other(col, d)})
    greet({"col": partner})

    own_copy = pltpu.make_async_copy(src_hbm, own, own_sem)
    own_copy.start()
    right_copy = pltpu.make_async_copy(right_hbm, right, far_sem.at[0])
    left_copy = pltpu.make_async_copy(left_hbm, left, far_sem.at[1])
    right_copy.start()
    left_copy.start()

    def near_copy(i):
        return pltpu.make_async_copy(near_hbm.at[i], tiles.at[i], near_sem.at[i])

    def theirs(t):
        return 2 * t + 1 - core

    def ours(s):
        q = s // 2
        dz = jnp.where(q == 0, 2, jnp.where(q == 1, 1, jnp.where(q == 2, 3, 0)))
        dy = 1 - lax.rem(s, 2)
        z, y = chip // 2, lax.rem(chip, 2)
        return lax.rem(z + dz, planes) * 2 + lax.rem(y + dy, 2)

    @pl.loop(0, chips)
    def _(t):
        near_copy(theirs(t)).start()

    @pl.loop(0, chips)
    def _(s):
        near_copy(2 * ours(s) + core).start()

    pl.semaphore_wait(barrier, n_row - 1 + chips)

    def to_row(k, src, dst, send, recv):
        return pltpu.make_async_remote_copy(
            src_ref=src, dst_ref=dst, send_sem=send, recv_sem=recv,
            device_id={"row": k}, device_id_type=MESH,
        )

    def to_col(c, src, dst, send, recv):
        return pltpu.make_async_remote_copy(
            src_ref=src, dst_ref=dst, send_sem=send, recv_sem=recv,
            device_id={"col": c}, device_id_type=MESH,
        )

    def give(block, origin, device, slot):
        return to_col(device, block, row_src.at[origin], gr_send.at[slot], gr_recv.at[origin])

    def got(origin):
        give(own, origin, partner, 0).wait_recv()

    own_copy.wait()

    @pl.loop(0, row)
    def _(k):
        to_row(k, own, col_src.at[row], gc_send.at[k], gc_recv.at[row]).start()

    @pl.loop(1, chips)
    def _(d):
        give(own, col, other(col, d), d).start()

    give(own, col, partner, 0).start()

    col_src[row] = own[...]
    row_src[col] = own[...]

    @pl.loop(0, row)
    def _(k):
        col_src[k] = jnp.zeros_like(own)

    def weight(i, k, kind):
        big_i, big_j = row * n_col + i, k * n_col + col
        ok = (big_i <= big_j) & (big_j <= band_ref[i]) & (pat_ref[k, i] == kind)
        return jnp.where(ok, 1.0, 0.0).astype(F32)

    lane = lax.broadcasted_iota(jnp.int32, (1, LANES), 1) // rank
    wide_lane = lax.broadcasted_iota(jnp.int32, (num_cases, LANES), 1) // rank

    def lay(parts, place):
        total = parts[-1]
        for p in range(per - 1):
            total = jnp.where(place == p, parts[p], total)
        return total

    @pl.loop(0, n_col // per)
    def _(g):
        for kk in range(n_row // per):
            far = {}
            for t in range(per):
                for s in range(per):
                    i, k = g * per + t, kk * per + s
                    far[t, s] = jnp.full((1, LANES), weight(i, k, 2), F32)
                    near_keep[i * n_row + k] = weight(i, k, 1)
            for t in range(per):
                fwd_keep[g * per + t, kk] = lay([far[t, (p - t) % per] for p in range(per)], lane)
            for s in range(per):
                bwd_keep[kk * per + s, g] = lay([far[(p - s) % per, s] for p in range(per)], lane)

    def turn(i):
        near_copy(i).wait()
        for k in range(n_row):
            turned[i, k] = tiles[i, k].T

    @pl.loop(0, chips)
    def _(t):
        turn(theirs(t))

    @pl.loop(0, chips)
    def _(s):
        turn(2 * ours(s) + core)

    @pl.loop(row + 1, n_row)
    def _(k):
        to_row(row, own, col_src.at[k], gc_send.at[row], gc_recv.at[k]).wait_recv()

    right_copy.wait()
    for kk in range(n_row // per):
        for gp in range(n_col // per // 2):
            coef = []
            for s in range(per):
                k = kk * per + s
                rows = [
                    right[(gp * 2 + g) * per + (p - s) % per, k] for g in range(2) for p in range(per)
                ]
                coef.append(dot_nt(col_src[k], jnp.concatenate(rows, axis=0)))
            for g in range(2):
                for t in range(per):
                    i = (gp * 2 + g) * per + t
                    piece = lay(
                        [coef[(p - t) % per][:, g * LANES:(g + 1) * LANES] for p in range(per)],
                        wide_lane,
                    )
                    fwd[i, kk] = (piece * fwd_keep[i, kk]).astype(BF16)

    @pl.loop(1, chips)
    def _(d):
        origin = other(col, d)
        got(origin)
        give(row_src.at[origin], origin, partner, chips - 1 + d).start()

    left_copy.wait()

    def left_rows(i):
        return jnp.concatenate(
            [
                left[i, kk * per + lax.rem(p - i + n_col, per)]
                for kk in range(n_row // per)
                for p in range(per)
            ],
            axis=0,
        )

    def row_term(i):
        acc = dot_nn(
            jnp.concatenate([fwd[i, kk] for kk in range(n_row // per)], axis=1), left_rows(i)
        )
        for k in range(n_row):
            acc += dot_nn(col_src[k] * near_keep[i * n_row + k].astype(BF16), turned[i, k])
        return acc

    def pair_copy(t):
        return to_col(partner, pair_send.at[t], pair_recv.at[t], pa_send.at[t], pa_recv.at[t])

    def row_copy(t):
        return to_col(
            2 * t + core, row_send.at[t], row_recv.at[chip], rr_send.at[t], rr_recv.at[chip]
        )

    @pl.loop(0, chips // 2)
    def _(h):
        terms = [row_term(theirs(2 * h + u)) for u in range(2)]
        for u in range(2):
            pair_send[2 * h + u] = terms[u]
        for u in range(2):
            pair_copy(2 * h + u).start()

    @pl.loop(0, chips // 2)
    def _(h):
        terms = [row_term(2 * ours(2 * h + u) + core) for u in range(2)]
        for u in range(2):
            t = ours(2 * h + u)
            pair_copy(t).wait_recv()
            acc = terms[u] + pair_recv[t]

            @pl.when(t == chip)
            def _():
                out_ref[...] = acc

            @pl.when(t != chip)
            def _():
                row_send[t] = acc.astype(BF16)
                row_copy(t).start()

    @pl.loop(0, chips)
    def _(d):
        got(other(partner, d))

    for g in range(n_col // per):
        back = [dot_nt(row_src[g * per + t], left_rows(g * per + t)) for t in range(per)]
        for kk in range(n_row // per):
            for s in range(per):
                k = kk * per + s
                piece = lay(
                    [back[(p - s) % per][:, kk * LANES:(kk + 1) * LANES] for p in range(per)],
                    wide_lane,
                )
                bwd[k, g] = (piece * bwd_keep[k, g]).astype(BF16)

    def col_copy(k):
        return to_row(k, col_send.at[k], col_recv.at[row], rc_send.at[k], rc_recv.at[row])

    def col_term(k):
        acc = jnp.zeros((num_cases, size), F32)
        for h in range(n_col // per // 2):
            rows = [
                right[(h * 2 + g) * per + lax.rem(p - k + n_row, per), k]
                for g in range(2)
                for p in range(per)
            ]
            acc += dot_nn(
                jnp.concatenate([bwd[k, h * 2], bwd[k, h * 2 + 1]], axis=1),
                jnp.concatenate(rows, axis=0),
            )
        for i in range(n_col):
            acc += dot_nn(row_src[i] * near_keep[i * n_row + k].astype(BF16), tiles[i, k])
        return acc

    @pl.loop(0, n_row // 2)
    def _(step):
        high = n_row - 1 - 2 * step

        @pl.when(high >= row)
        def _():
            terms = [col_term(high - u) for u in range(2)]
            for u in range(2):
                k, acc = high - u, terms[u]

                @pl.when(k == row)
                def _():
                    out_ref[...] += acc

                @pl.when(k > row)
                def _():
                    col_send[k] = acc.astype(BF16)
                    col_copy(k).start()

    @pl.loop(1, chips)
    def _(d):
        t = lax.rem(chip + d, chips)
        to_col(col, own, row_recv.at[t], rr_send.at[chip], rr_recv.at[t]).wait_recv()
        out_ref[...] += row_recv[t].astype(F32)

    @pl.loop(0, row)
    def _(k):
        to_row(row, own, col_recv.at[k], rc_send.at[row], rc_recv.at[k]).wait_recv()
        out_ref[...] += col_recv[k].astype(F32)

    @pl.loop(0, n_col - 1)
    def _(slot):
        give(own, col, partner, slot).wait_send()

    @pl.loop(0, chips)
    def _(t):
        pair_copy(t).wait_send()

    @pl.loop(1, chips)
    def _(d):
        row_copy(lax.rem(chip + d, chips)).wait_send()

    @pl.loop(0, row)
    def _(k):
        to_row(k, own, col_src.at[row], gc_send.at[k], gc_recv.at[row]).wait_send()

    @pl.loop(row + 1, n_row)
    def _(k):
        col_copy(k).wait_send()


def shards(sources, near_tiles, far_left, far_right, pattern, band_end):
    n_col, n_row, size = near_tiles.shape[:3]
    rank = far_left.shape[2]
    cases = sources.shape[0]
    per = LANES // rank
    dma = pltpu.SemaphoreType.DMA
    hbm = pl.BlockSpec(memory_space=pltpu.HBM)
    smem = pl.BlockSpec(memory_space=pltpu.SMEM)
    return pl.pallas_call(
        kernel,
        out_shape=jax.ShapeDtypeStruct((cases, size), F32),
        in_specs=[hbm, hbm, hbm, hbm, smem, smem],
        out_specs=pl.BlockSpec(memory_space=pltpu.VMEM),
        scratch_shapes=[
            pltpu.VMEM(near_tiles.shape, BF16),
            pltpu.VMEM(near_tiles.shape, BF16),
            pltpu.VMEM(far_left.shape, BF16),
            pltpu.VMEM(far_right.shape, BF16),
            pltpu.VMEM((cases, size), BF16),
            pltpu.VMEM((n_col, cases, size), BF16),
            pltpu.VMEM((n_row, cases, size), BF16),
            pltpu.VMEM((n_col, n_row // per, cases, LANES), BF16),
            pltpu.VMEM((n_row, n_col // per, cases, LANES), BF16),
            pltpu.VMEM((n_col, n_row // per, 1, LANES), F32),
            pltpu.VMEM((n_row, n_col // per, 1, LANES), F32),
            pltpu.SMEM((n_col * n_row,), F32),
            pltpu.VMEM((n_col // 2, cases, size), F32),
            pltpu.VMEM((n_col // 2, cases, size), F32),
            pltpu.VMEM((n_col // 2, cases, size), BF16),
            pltpu.VMEM((n_col // 2, cases, size), BF16),
            pltpu.VMEM((n_row, cases, size), BF16),
            pltpu.VMEM((n_row, cases, size), BF16),
            dma,
            dma((n_col,)),
            dma((2,)),
            dma((n_col - 1,)), dma((n_col,)),
            dma((n_row,)), dma((n_row,)),
            dma((n_col // 2,)), dma((n_col // 2,)),
            dma((n_col // 2,)), dma((n_col // 2,)),
            dma((n_row,)), dma((n_row,)),
        ],
        compiler_params=pltpu.CompilerParams(
            collective_id=0, has_side_effects=True, vmem_limit_bytes=60 * 1024 * 1024
        ),
        name="panels",
    )(sources, near_tiles, far_left, far_right, pattern.T, band_end)


def solution(mesh):
    placed = (
        P(None, ("row", "col")),
        P("row", "col", None, None),
        P("row", "col", None, None),
        P("row", "col", None, None),
        P("row", "col"),
        P("row"),
    )
    return jax.shard_map(
        shards, mesh=mesh, in_specs=placed, out_specs=P(None, ("row", "col")), check_vma=False
    )
```

time: 38 us -> 30.3 us (0.80)
  the two profiles are of different devices: /device:TPU:2 before, /device:TPU:8 now
where the time goes in v2:
time: 30.3 us; the launch traced here: 30.1 us
  Pallas kernels  28.6 us (94%)
  local copies, waits for them, and re-layouts  1.47 us (5%)
    pallas_call x1, Pallas kernels, shards(): pl.pallas_call(kernel, out_shape=jax.ShapeDtypeStruct((cases, size), F32)...  28.6 us
    unnamed x1, local copies, waits for them, and re-layouts  1.47 us

profile of v2, /device:TPU:8, one launch (start us, length us, event | category | flops | bytes accessed | tf_op | source)
XLA Modules:
  0.0 30.1 jit_solution(15112032890737853056)
XLA Ops:
  0.0 28.6 %panels.1 = f32[64,256]{1,0:T(8,128)} custom-call(bf16[64,256]{1,0:T(8,128)(2,1)} %src_hbm.1, bf16[16,8,256,256]{3,2,1,0:T(8,128)(2,1)} %near_hbm.1, bf16[16,8,32,256]{3,2,1,0:T(8,128)(2,1)} %left_hbm.1, bf16[16,8,32,256]{3,2,1,0:T(8,128)(2,1)} %right_hbm.1, s32[8,16]{1,0:T(8,128)} %bitcast.1, s32[16]{0:T(128)} %band_ref.1), custom_call_target="tpu_custom_call" | custom-call | tf_op jit(solution)/shard_map/panels/pallas_call | solution.py:338
  28.7 1.5 %copy.8 = f32[64,256]{1,0:T(8,128)} copy(f32[64,256]{1,0:T(8,128)} %panels.1) | data formatting | bytes 131072

commit v3 on v2

--- a/solution.py
+++ b/solution.py
@@ -28,7 +28,7 @@
     own_sem, near_sem, far_sem, gr_send, gr_recv, gc_send, gc_recv,
     pa_send, pa_recv, rr_send, rr_recv, rc_send, rc_recv,
 ):
-    n_row, n_col = near_hbm.shape[1], near_hbm.shape[0]
+    n_row, n_col = near_hbm.shape[2], 2 * near_hbm.shape[0]
     rank = left_hbm.shape[2]
     num_cases, size = own.shape
     per = LANES // rank
@@ -41,26 +41,32 @@
     def other(c, d):
         return lax.rem(c + 2 * d, n_col)
 
+    own_copy = pltpu.make_async_copy(src_hbm, own, own_sem)
+    own_copy.start()
+
     barrier = pltpu.get_barrier_semaphore()
 
     def greet(device):
         pl.semaphore_signal(barrier, inc=1, device_id=device, device_id_type=MESH)
 
+    for d in range(1, chips):
+        greet({"col": other(col, d)})
     for d in range(1, n_row):
         greet({"row": lax.rem(row + d, n_row)})
-    for d in range(1, chips):
-        greet({"col": other(col, d)})
     greet({"col": partner})
 
-    own_copy = pltpu.make_async_copy(src_hbm, own, own_sem)
-    own_copy.start()
     right_copy = pltpu.make_async_copy(right_hbm, right, far_sem.at[0])
     left_copy = pltpu.make_async_copy(left_hbm, left, far_sem.at[1])
     right_copy.start()
     left_copy.start()
 
-    def near_copy(i):
-        return pltpu.make_async_copy(near_hbm.at[i], tiles.at[i], near_sem.at[i])
+    quarter = chips // 2
+
+    def near_copy(side, part):
+        span = pl.ds(part * quarter, quarter)
+        return pltpu.make_async_copy(
+            near_hbm.at[span, side], tiles.at[span, side], near_sem.at[side, part]
+        )
 
     def theirs(t):
         return 2 * t + 1 - core
@@ -72,13 +78,9 @@
         z, y = chip // 2, lax.rem(chip, 2)
         return lax.rem(z + dz, planes) * 2 + lax.rem(y + dy, 2)
 
-    @pl.loop(0, chips)
-    def _(t):
-        near_copy(theirs(t)).start()
-
-    @pl.loop(0, chips)
-    def _(s):
-        near_copy(2 * ours(s) + core).start()
+    for side in (1 - core, core):
+        for part in range(2):
+            near_copy(side, part).start()
 
     pl.semaphore_wait(barrier, n_row - 1 + chips)
 
@@ -147,18 +149,23 @@
             for s in range(per):
                 bwd_keep[kk * per + s, g] = lay([far[(p - s) % per, s] for p in range(per)], lane)
 
-    def turn(i):
-        near_copy(i).wait()
+    def turn(t, side):
         for k in range(n_row):
-            turned[i, k] = tiles[i, k].T
-
-    @pl.loop(0, chips)
-    def _(t):
-        turn(theirs(t))
-
-    @pl.loop(0, chips)
+            turned[t, side, k] = tiles[t, side, k].T
+
+    for part in range(2):
+        near_copy(1 - core, part).wait()
+
+        @pl.loop(part * quarter, (part + 1) * quarter)
+        def _(t):
+            turn(t, 1 - core)
+
+    for part in range(2):
+        near_copy(core, part).wait()
+
+    @pl.loop(0, quarter)
     def _(s):
-        turn(2 * ours(s) + core)
+        turn(ours(s), core)
 
     @pl.loop(row + 1, n_row)
     def _(k):
@@ -206,7 +213,7 @@
             jnp.concatenate([fwd[i, kk] for kk in range(n_row // per)], axis=1), left_rows(i)
         )
         for k in range(n_row):
-            acc += dot_nn(col_src[k] * near_keep[i * n_row + k].astype(BF16), turned[i, k])
+            acc += dot_nn(col_src[k] * near_keep[i * n_row + k].astype(BF16), turned[i // 2, lax.rem(i, 2), k])
         return acc
 
     def pair_copy(t):
@@ -220,6 +227,7 @@
     @pl.loop(0, chips // 2)
     def _(h):
         terms = [row_term(theirs(2 * h + u)) for u in range(2)]
+        turn(ours(quarter + h), core)
         for u in range(2):
             pair_send[2 * h + u] = terms[u]
         for u in range(2):
@@ -273,7 +281,7 @@
                 jnp.concatenate(rows, axis=0),
             )
         for i in range(n_col):
-            acc += dot_nn(row_src[i] * near_keep[i * n_row + k].astype(BF16), tiles[i, k])
+            acc += dot_nn(row_src[i] * near_keep[i * n_row + k].astype(BF16), tiles[i // 2, i % 2, k])
         return acc
 
     @pl.loop(0, n_row // 2)
@@ -303,8 +311,9 @@
 
     @pl.loop(0, row)
     def _(k):
-        to_row(row, own, col_recv.at[k], rc_send.at[row], rc_recv.at[k]).wait_recv()
-        out_ref[...] += col_recv[k].astype(F32)
+        last = row - 1 - k
+        to_row(row, own, col_recv.at[last], rc_send.at[row], rc_recv.at[last]).wait_recv()
+        out_ref[...] += col_recv[last].astype(F32)
 
     @pl.loop(0, n_col - 1)
     def _(slot):
@@ -332,6 +341,7 @@
     rank = far_left.shape[2]
     cases = sources.shape[0]
     per = LANES // rank
+    pairs = near_tiles.reshape(n_col // 2, 2, n_row, size, size)
     dma = pltpu.SemaphoreType.DMA
     hbm = pl.BlockSpec(memory_space=pltpu.HBM)
     smem = pl.BlockSpec(memory_space=pltpu.SMEM)
@@ -341,8 +351,8 @@
         in_specs=[hbm, hbm, hbm, hbm, smem, smem],
         out_specs=pl.BlockSpec(memory_space=pltpu.VMEM),
         scratch_shapes=[
-            pltpu.VMEM(near_tiles.shape, BF16),
-            pltpu.VMEM(near_tiles.shape, BF16),
+            pltpu.VMEM(pairs.shape, BF16),
+            pltpu.VMEM(pairs.shape, BF16),
             pltpu.VMEM(far_left.shape, BF16),
             pltpu.VMEM(far_right.shape, BF16),
             pltpu.VMEM((cases, size), BF16),
@@ -360,7 +370,7 @@
             pltpu.VMEM((n_row, cases, size), BF16),
             pltpu.VMEM((n_row, cases, size), BF16),
             dma,
-            dma((n_col,)),
+            dma((2, 2)),
             dma((2,)),
             dma((n_col - 1,)), dma((n_col,)),
             dma((n_row,)), dma((n_row,)),
@@ -372,7 +382,7 @@
             collective_id=0, has_side_effects=True, vmem_limit_bytes=60 * 1024 * 1024
         ),
         name="panels",
-    )(sources, near_tiles, far_left, far_right, pattern.T, band_end)
+    )(sources, pairs, far_left, far_right, pattern.T, band_end)
 
 
 def solution(mesh):

time: 30.3 us -> 29 us (0.957)
  Pallas kernels: 28.6 us -> 27.3 us
    pallas_call x1, Pallas kernels: 28.6 us -> 27.3 us  [shards(): pl.pallas_call(kernel, out_shape=jax.ShapeDtypeStruct((cases, size), F32)...]
where the time goes in v3:
time: 29 us; the launch traced here: 28.8 us
  Pallas kernels  27.3 us (94%)
  local copies, waits for them, and re-layouts  1.47 us (5%)
    pallas_call x1, Pallas kernels, shards(): pl.pallas_call(kernel, out_shape=jax.ShapeDtypeStruct((cases, size), F32)...  27.3 us
    unnamed x1, local copies, waits for them, and re-layouts  1.47 us

profile of v3, /device:TPU:8, one launch (start us, length us, event | category | flops | bytes accessed | tf_op | source)
XLA Modules:
  0.0 28.8 jit_solution(5722671497831039585)
XLA Ops:
  0.0 27.3 %panels.1 = f32[64,256]{1,0:T(8,128)} custom-call(bf16[64,256]{1,0:T(8,128)(2,1)} %src_hbm.1, bf16[8,2,8,256,256]{4,3,2,1,0:T(8,128)(2,1)} %bitcast.2, bf16[16,8,32,256]{3,2,1,0:T(8,128)(2,1)} %left_hbm.1, bf16[16,8,32,256]{3,2,1,0:T(8,128)(2,1)} %right_hbm.1, s32[8,16]{1,0:T(8,128)} %bitcast.3, s32[16]{0:T(128)} %band_ref.1), custom_call_target="tpu_custom_call" | custom-call | tf_op jit(solution)/shard_map/panels/pallas_call | solution.py:348
  27.3 1.5 %copy.8 = f32[64,256]{1,0:T(8,128)} copy(f32[64,256]{1,0:T(8,128)} %panels.1) | data formatting | bytes 131072

commit v4 on v3

--- a/solution.py
+++ b/solution.py
@@ -25,7 +25,7 @@
     src_hbm, near_hbm, left_hbm, right_hbm, pat_ref, band_ref, out_ref,
     tiles, turned, left, right, own, row_src, col_src, fwd, bwd, fwd_keep, bwd_keep, near_keep,
     pair_send, pair_recv, row_send, row_recv, col_send, col_recv,
-    own_sem, near_sem, far_sem, gr_send, gr_recv, gc_send, gc_recv,
+    row_open, col_open, own_sem, near_sem, far_sem, gr_send, gr_recv, gc_send, gc_recv,
     pa_send, pa_recv, rr_send, rr_recv, rc_send, rc_recv,
 ):
     n_row, n_col = near_hbm.shape[2], 2 * near_hbm.shape[0]
@@ -49,16 +49,19 @@
     def greet(device):
         pl.semaphore_signal(barrier, inc=1, device_id=device, device_id_type=MESH)
 
+    @pl.loop(row + 1, n_row)
+    def _(k):
+        greet({"row": k, "col": col - core})
+
+    @pl.when(core == 1)
+    def _():
+        greet({"col": partner})
+
     for d in range(1, chips):
-        greet({"col": other(col, d)})
-    for d in range(1, n_row):
-        greet({"row": lax.rem(row + d, n_row)})
-    greet({"col": partner})
+        greet({"col": other(col - core + 1, d)})
 
     right_copy = pltpu.make_async_copy(right_hbm, right, far_sem.at[0])
     left_copy = pltpu.make_async_copy(left_hbm, left, far_sem.at[1])
-    right_copy.start()
-    left_copy.start()
 
     quarter = chips // 2
 
@@ -78,11 +81,22 @@
         z, y = chip // 2, lax.rem(chip, 2)
         return lax.rem(z + dz, planes) * 2 + lax.rem(y + dy, 2)
 
-    for side in (1 - core, core):
+    first = 1 - core
+    for side in (first, core):
         for part in range(2):
             near_copy(side, part).start()
-
-    pl.semaphore_wait(barrier, n_row - 1 + chips)
+            if side is first and part == 0:
+                right_copy.start()
+                left_copy.start()
+
+    @pl.when(core == 0)
+    def _():
+        pl.semaphore_wait(barrier, 2 * row + 1)
+        pl.semaphore_signal(row_open, inc=1, device_id={"col": partner}, device_id_type=MESH)
+
+    @pl.when(core == 1)
+    def _():
+        pl.semaphore_wait(row_open, 1)
 
     def to_row(k, src, dst, send, recv):
         return pltpu.make_async_remote_copy(
@@ -107,10 +121,6 @@
     @pl.loop(0, row)
     def _(k):
         to_row(k, own, col_src.at[row], gc_send.at[k], gc_recv.at[row]).start()
-
-    @pl.loop(1, chips)
-    def _(d):
-        give(own, col, other(col, d), d).start()
 
     give(own, col, partner, 0).start()
 
@@ -153,7 +163,26 @@
         for k in range(n_row):
             turned[t, side, k] = tiles[t, side, k].T
 
-    for part in range(2):
+    near_copy(1 - core, 0).wait()
+
+    @pl.loop(0, quarter)
+    def _(t):
+        turn(t, 1 - core)
+
+    @pl.when(core == 1)
+    def _():
+        pl.semaphore_wait(barrier, 2 * (chips - 1))
+        pl.semaphore_signal(col_open, inc=1, device_id={"col": partner}, device_id_type=MESH)
+
+    @pl.when(core == 0)
+    def _():
+        pl.semaphore_wait(col_open, 1)
+
+    @pl.loop(1, chips)
+    def _(d):
+        give(own, col, other(col, d), d).start()
+
+    for part in range(1, 2):
         near_copy(1 - core, part).wait()
 
         @pl.loop(part * quarter, (part + 1) * quarter)
@@ -190,12 +219,6 @@
                     )
                     fwd[i, kk] = (piece * fwd_keep[i, kk]).astype(BF16)
 
-    @pl.loop(1, chips)
-    def _(d):
-        origin = other(col, d)
-        got(origin)
-        give(row_src.at[origin], origin, partner, chips - 1 + d).start()
-
     left_copy.wait()
 
     def left_rows(i):
@@ -232,6 +255,12 @@
             pair_send[2 * h + u] = terms[u]
         for u in range(2):
             pair_copy(2 * h + u).start()
+
+    @pl.loop(1, chips)
+    def _(d):
+        origin = other(col, d)
+        got(origin)
+        give(row_src.at[origin], origin, partner, chips - 1 + d).start()
 
     @pl.loop(0, chips // 2)
     def _(h):
@@ -369,6 +398,8 @@
             pltpu.VMEM((n_col // 2, cases, size), BF16),
             pltpu.VMEM((n_row, cases, size), BF16),
             pltpu.VMEM((n_row, cases, size), BF16),
+            pltpu.SemaphoreType.REGULAR,
+            pltpu.SemaphoreType.REGULAR,
             dma,
             dma((2, 2)),
             dma((2,)),

time: 29 us -> 27.3 us (0.941)
  Pallas kernels: 27.3 us -> 25.6 us
    pallas_call x1, Pallas kernels: 27.3 us -> 25.6 us  [shards(): pl.pallas_call(kernel, out_shape=jax.ShapeDtypeStruct((cases, size), F32)...]
where the time goes in v4:
time: 27.3 us; the launch traced here: 27.1 us
  Pallas kernels  25.6 us (94%)
  local copies, waits for them, and re-layouts  1.47 us (5%)
    pallas_call x1, Pallas kernels, shards(): pl.pallas_call(kernel, out_shape=jax.ShapeDtypeStruct((cases, size), F32)...  25.6 us
    unnamed x1, local copies, waits for them, and re-layouts  1.47 us

profile of v4, /device:TPU:8, one launch (start us, length us, event | category | flops | bytes accessed | tf_op | source)
XLA Modules:
  0.0 27.1 jit_solution(6619975048081484309)
XLA Ops:
  0.0 25.6 %panels.1 = f32[64,256]{1,0:T(8,128)} custom-call(bf16[64,256]{1,0:T(8,128)(2,1)} %src_hbm.1, bf16[8,2,8,256,256]{4,3,2,1,0:T(8,128)(2,1)} %bitcast.2, bf16[16,8,32,256]{3,2,1,0:T(8,128)(2,1)} %left_hbm.1, bf16[16,8,32,256]{3,2,1,0:T(8,128)(2,1)} %right_hbm.1, s32[8,16]{1,0:T(8,128)} %bitcast.3, s32[16]{0:T(128)} %band_ref.1), custom_call_target="tpu_custom_call" | custom-call | tf_op jit(solution)/shard_map/panels/pallas_call | solution.py:377
  25.6 1.5 %copy.8 = f32[64,256]{1,0:T(8,128)} copy(f32[64,256]{1,0:T(8,128)} %panels.1) | data formatting | bytes 131072

commit v5 on v4

--- a/solution.py
+++ b/solution.py
@@ -181,6 +181,7 @@
     @pl.loop(1, chips)
     def _(d):
         give(own, col, other(col, d), d).start()
+        give(own, col, other(partner, d), chips - 1 + d).start()
 
     for part in range(1, 2):
         near_copy(1 - core, part).wait()
@@ -201,6 +202,7 @@
         to_row(row, own, col_src.at[k], gc_send.at[row], gc_recv.at[k]).wait_recv()
 
     right_copy.wait()
+    left_copy.wait()
     for kk in range(n_row // per):
         for gp in range(n_col // per // 2):
             coef = []
@@ -219,7 +221,6 @@
                     )
                     fwd[i, kk] = (piece * fwd_keep[i, kk]).astype(BF16)
 
-    left_copy.wait()
 
     def left_rows(i):
         return jnp.concatenate(
@@ -247,8 +248,7 @@
             2 * t + core, row_send.at[t], row_recv.at[chip], rr_send.at[t], rr_recv.at[chip]
         )
 
-    @pl.loop(0, chips // 2)
-    def _(h):
+    def pass_on(h):
         terms = [row_term(theirs(2 * h + u)) for u in range(2)]
         turn(ours(quarter + h), core)
         for u in range(2):
@@ -256,11 +256,8 @@
         for u in range(2):
             pair_copy(2 * h + u).start()
 
-    @pl.loop(1, chips)
-    def _(d):
-        origin = other(col, d)
-        got(origin)
-        give(row_src.at[origin], origin, partner, chips - 1 + d).start()
+    pass_on(0)
+    pl.loop(1, chips // 2)(pass_on)
 
     @pl.loop(0, chips // 2)
     def _(h):
@@ -282,6 +279,10 @@
     @pl.loop(0, chips)
     def _(d):
         got(other(partner, d))
+
+    @pl.loop(1, chips)
+    def _(d):
+        got(other(col, d))
 
     for g in range(n_col // per):
         back = [dot_nt(row_src[g * per + t], left_rows(g * per + t)) for t in range(per)]
@@ -313,24 +314,29 @@
             acc += dot_nn(row_src[i] * near_keep[i * n_row + k].astype(BF16), tiles[i // 2, i % 2, k])
         return acc
 
-    @pl.loop(0, n_row // 2)
+    def col_pair(high):
+        terms = [col_term(high - u) for u in range(2)]
+        for u in range(2):
+            k, acc = high - u, terms[u]
+
+            @pl.when(k == row)
+            def _():
+                out_ref[...] += acc
+
+            @pl.when(k > row)
+            def _():
+                col_send[k] = acc.astype(BF16)
+                col_copy(k).start()
+
+    col_pair(n_row - 1)
+
+    @pl.loop(1, n_row // 2)
     def _(step):
         high = n_row - 1 - 2 * step
 
         @pl.when(high >= row)
         def _():
-            terms = [col_term(high - u) for u in range(2)]
-            for u in range(2):
-                k, acc = high - u, terms[u]
-
-                @pl.when(k == row)
-                def _():
-                    out_ref[...] += acc
-
-                @pl.when(k > row)
-                def _():
-                    col_send[k] = acc.astype(BF16)
-                    col_copy(k).start()
+            col_pair(high)
 
     @pl.loop(1, chips)
     def _(d):

time: 27.3 us -> 27.1 us (level)
  Pallas kernels: 25.6 us -> 25.3 us
    pallas_call x1, Pallas kernels: 25.6 us -> 25.3 us  [shards(): pl.pallas_call(kernel, out_shape=jax.ShapeDtypeStruct((cases, size), F32)...]
where the time goes in v5:
time: 27.1 us; the launch traced here: 26.8 us
  Pallas kernels  25.3 us (93%)
  local copies, waits for them, and re-layouts  1.47 us (5%)
    pallas_call x1, Pallas kernels, shards(): pl.pallas_call(kernel, out_shape=jax.ShapeDtypeStruct((cases, size), F32)...  25.3 us
    unnamed x1, local copies, waits for them, and re-layouts  1.47 us

profile of v5, /device:TPU:8, one launch (start us, length us, event | category | flops | bytes accessed | tf_op | source)
XLA Modules:
  0.0 26.8 jit_solution(5083598138686940061)
XLA Ops:
  0.0 25.3 %panels.1 = f32[64,256]{1,0:T(8,128)} custom-call(bf16[64,256]{1,0:T(8,128)(2,1)} %src_hbm.1, bf16[8,2,8,256,256]{4,3,2,1,0:T(8,128)(2,1)} %bitcast.2, bf16[16,8,32,256]{3,2,1,0:T(8,128)(2,1)} %left_hbm.1, bf16[16,8,32,256]{3,2,1,0:T(8,128)(2,1)} %right_hbm.1, s32[8,16]{1,0:T(8,128)} %bitcast.3, s32[16]{0:T(128)} %band_ref.1), custom_call_target="tpu_custom_call" | custom-call | tf_op jit(solution)/shard_map/panels/pallas_call | solution.py:383
  25.3 1.5 %copy.8 = f32[64,256]{1,0:T(8,128)} copy(f32[64,256]{1,0:T(8,128)} %panels.1) | data formatting | bytes 131072

commit v6 on v5

--- a/solution.py
+++ b/solution.py
@@ -85,9 +85,8 @@
     for side in (first, core):
         for part in range(2):
             near_copy(side, part).start()
-            if side is first and part == 0:
-                right_copy.start()
-                left_copy.start()
+    right_copy.start()
+    left_copy.start()
 
     @pl.when(core == 0)
     def _():

time: 27.1 us -> 27 us (level)
  no operation moved by 1% of the time
where the time goes in v6:
time: 27 us; the launch traced here: 26.8 us
  Pallas kernels  25.3 us (94%)
  local copies, waits for them, and re-layouts  1.47 us (5%)
    pallas_call x1, Pallas kernels, shards(): pl.pallas_call(kernel, out_shape=jax.ShapeDtypeStruct((cases, size), F32)...  25.3 us
    unnamed x1, local copies, waits for them, and re-layouts  1.47 us

profile of v6, /device:TPU:8, one launch (start us, length us, event | category | flops | bytes accessed | tf_op | source)
XLA Modules:
  0.0 26.8 jit_solution(279680447588957118)
XLA Ops:
  0.0 25.3 %panels.1 = f32[64,256]{1,0:T(8,128)} custom-call(bf16[64,256]{1,0:T(8,128)(2,1)} %src_hbm.1, bf16[8,2,8,256,256]{4,3,2,1,0:T(8,128)(2,1)} %bitcast.2, bf16[16,8,32,256]{3,2,1,0:T(8,128)(2,1)} %left_hbm.1, bf16[16,8,32,256]{3,2,1,0:T(8,128)(2,1)} %right_hbm.1, s32[8,16]{1,0:T(8,128)} %bitcast.3, s32[16]{0:T(128)} %band_ref.1), custom_call_target="tpu_custom_call" | custom-call | tf_op jit(solution)/shard_map/panels/pallas_call | solution.py:382
  25.3 1.5 %copy.8 = f32[64,256]{1,0:T(8,128)} copy(f32[64,256]{1,0:T(8,128)} %panels.1) | data formatting | bytes 131072
